TPU v7x, 32 devices: a whole 2x2x4 slice. The times are simulated.
32 devices in a mesh: groups: 2 (over y), seq: 4 (over z), head: 4 (over x, core).
Axes of the slice: x: 2, y: 2, z: 4, core: 2. Of those that a mesh axis runs over, the one named last changes fastest.
Arguments:
- query_latent_rows: bfloat16 [640, 1536], P(('groups', 'seq')), parts along dimension 0, may hold values from -6 to 6
- key_value_latents: bfloat16 [640, 576], P(('groups', 'seq')), parts along dimension 0, may hold values from -500 to 500
- positions: int32 [640], P(('groups', 'seq')), parts along dimension 0, may hold values from 130752 to 131071, as said below
- query_up_weight: bfloat16 [1536, 12288], P('seq', 'head'), may hold values from -0.15625 to 0.15625
- adapter_down_factor: bfloat16 [3072, 64], P(('groups', 'seq')), parts along dimension 0, may hold values from -0.75 to 0.75
- adapter_up_factor: bfloat16 [128, 12288], P('groups', 'head'), parts along dimension 0, may hold values from -0.15625 to 0.15625
- head_key_up_weight: bfloat16 [64, 128, 512], P('head'), may hold values from -0.5 to 0.5
- head_value_up_weight: bfloat16 [64, 512, 128], P('head'), may hold values from -0.25 to 0.25
- output_projection_weight: bfloat16 [8192, 7168], P('head', 'seq'), may hold values from -0.0625 to 0.0625
Outputs:
- merged_weight: bfloat16 [3072, 12288], P(('groups', 'seq'), 'head'), parts along dimension 0
- mixed: bfloat16 [640, 7168], P(('groups', 'head'), 'seq'), parts along dimension 0
There are 2 independent parts, one for each index of `groups`. A program takes and returns all parts, laid end to end along the dimension named above; an argument that names none is the same for every part. Nothing has to cross between parts.
Inputs may be any that keep to these rules, and one draw needn't show every extreme that they name: positions are distinct; each aligned block of 80 rows holds 80 consecutive positions in rising order, and the blocks together cover the last 320 positions of the prompt in an order drawn from the seed.
All inputs are finite; a program needn't handle non-finite values.
Results may differ from a plain program's by a relative error of at most 0.015.
The roundings to bfloat16 on the way count: a program that leaves them out, or rounds other values in their place, can miss the bound.
Values may be sent and summed in bfloat16 or wider, within the bound.
A program may use at most 64 MiB of HBM per device.

v0:
```python
import math
import jax
import jax.numpy as jnp
from jax import lax
from jax.sharding import PartitionSpec as P


def on_device(
    query_latent_rows,
    key_value_latents,
    positions,
    query_up_weight,
    adapter_down_factor,
    adapter_up_factor,
    head_key_up_weight,
    head_value_up_weight,
    output_projection_weight,
):
    merged_query_weight = (
        query_up_weight.astype(jnp.float32)
        + jnp.dot(adapter_down_factor, adapter_up_factor, preferred_element_type=jnp.float32)
    ).astype(jnp.bfloat16)
    tok_rows = query_latent_rows.shape[0]
    queries = jnp.dot(
        query_latent_rows,
        lax.all_gather(merged_query_weight, "seq", axis=0, tiled=True),
        preferred_element_type=jnp.float32,
    )
    heads_dev = head_key_up_weight.shape[0]
    nope_dim = head_key_up_weight.shape[1]
    kv_rank = head_key_up_weight.shape[2]
    lat_width = key_value_latents.shape[1]
    score_scale = 1.0 / math.sqrt(nope_dim + lat_width - kv_rank)
    queries = queries.astype(jnp.bfloat16).reshape(tok_rows, heads_dev, -1)
    absorbed = jnp.einsum(
        "thn,hnk->thk",
        queries[:, :, :nope_dim],
        head_key_up_weight,
        preferred_element_type=jnp.float32,
    ).astype(jnp.bfloat16)
    full_query = jnp.concatenate([absorbed, queries[:, :, nope_dim:]], axis=2).reshape(
        tok_rows * heads_dev, lat_width
    )
    query_pos = jnp.repeat(positions, heads_dev)
    q_count = tok_rows * heads_dev
    row_max = jnp.full((q_count,), -1e30, jnp.float32)
    key_rows = lax.all_gather(key_value_latents, "seq", axis=0, tiled=True)
    key_pos = lax.all_gather(positions, "seq", axis=0, tiled=True)
    visible = key_pos[None, :] <= query_pos[:, None]
    scores = (
        lax.dot_general(
            full_query, key_rows, (((1,), (1,)), ((), ())), preferred_element_type=jnp.float32
        )
        * score_scale
    )
    scores = jnp.where(visible, scores, jnp.float32(-1e30))
    new_max = jnp.maximum(row_max, jnp.max(scores, axis=1))
    weights = jnp.where(visible, jnp.exp(scores - new_max[:, None]), jnp.float32(0.0))
    row_sum = jnp.sum(weights, axis=1)
    running = jnp.dot(
        weights.astype(jnp.bfloat16), key_rows[:, :kv_rank], preferred_element_type=jnp.float32
    )
    row_max, row_sum, running = (new_max, row_sum, running)
    context_output = (
        (running / row_sum[:, None]).astype(jnp.bfloat16).reshape(tok_rows, heads_dev, kv_rank)
    )
    heads_out = (
        jnp.einsum(
            "euw,uwz->euz", context_output, head_value_up_weight, preferred_element_type=jnp.float32
        )
        .astype(jnp.bfloat16)
        .reshape(tok_rows, -1)
    )
    partial_value = jnp.dot(
        lax.all_gather(heads_out, "seq", axis=0, tiled=True),
        output_projection_weight,
        preferred_element_type=jnp.float32,
    )
    mixed = lax.psum_scatter(
        partial_value.astype(jnp.bfloat16), "head", scatter_dimension=0, tiled=True
    )
    return (merged_query_weight, mixed)


def solution(mesh):
    placed = (
        P(("groups", "seq"), None),
        P(("groups", "seq"), None),
        P(("groups", "seq")),
        P("seq", "head"),
        P(("groups", "seq"), None),
        P("groups", "head"),
        P("head", None, None),
        P("head", None, None),
        P("head", "seq"),
    )
    return jax.shard_map(
        on_device,
        mesh=mesh,
        in_specs=placed,
        out_specs=(P(("groups", "seq"), "head"), P(("groups", "head"), "seq")),
        check_vma=False,
    )
```

profile of v0, /device:TPU:0, one launch (start us, length us, event | category | flops | bytes accessed | tf_op | source)
XLA Modules:
  0.0 269.0 jit_solution(17031424686050613375)
XLA Ops:
  7.2 4.2 %add_convert_fusion = bf16[384,3072]{1,0:T(8,128)(2,1)} fusion(bf16[384,3072]{1,0:T(8,128)(2,1)} %param.12, bf16[384,64]{0,1:T(8,128)(2,1)} %param.13, bf16[64,3072]{1,0:T(8,128)(2,1)} %param.14), kind=kOutput, calls=%fused_computation | convolution fusion | flops 154533888 | bytes 5160960 | tf_op jit(solution)/shard_map/dot_general | solution.py:21
  11.5 0.6 copy-done.5
  12.1 0.1 le.16
  12.2 0.6 dynamic-slice
  13.4 0.2 dynamic-update-slice
  13.7 9.9 %all-reduce = s32[320]{0:T(512)S(1)} all-reduce(s32[320]{0:T(512)S(1)} %dynamic-update-slice), channel_id=1, replica_groups=mesh['groups'=2,'seq'=4,'head'=4] {'seq'}, use_global_device_ids=true, to_apply=%add | all-reduce | flops 320 | bytes 2560
  23.6 25.1 %all_gather.14 = bf16[320,576]{1,0:T(8,128)(2,1)} all-gather(bf16[80,576]{1,0:T(8,128)(2,1)S(1)} %copy-done.4), channel_id=1, replica_groups=mesh['groups'=2,'seq'=4,'head'=4] {'seq'}, dimensions={0}, use_global_device_ids=true | all-gather | bytes 460800 | tf_op jit(solution)/shard_map/all_gather | solution.py:47
  48.7 137.6 %all-gather.3.cloned.1.call-done = bf16[1536,3072]{1,0:T(8,128)(2,1)} async-done(((bf16[384,3072]{1,0:T(8,128)(2,1)}), bf16[1536,3072]{1,0:T(8,128)(2,1)}) %all-gather.3.cloned.1.call-update) | async-done | bytes 9437200 | tf_op jit(solution)/shard_map/all_gather | solution.py:26
  186.3 5.4 %fusion = bf16[80,3072]{1,0:T(8,128)(2,1)S(1)} fusion(bf16[80,1536]{1,0:T(8,128)(2,1)S(1)} %copy-done.2, bf16[1536,3072]{1,0:T(8,128)(2,1)} %all-gather.3.cloned.1.call-done), kind=kOutput, calls=%fused_computation.2 | convolution fusion | flops 755220480 | bytes 10174464 | tf_op jit(solution)/shard_map/dot_general | solution.py:24
  191.8 0.7 reshape.22
  192.6 0.1 copy.20
  192.7 0.5 fusion.3
  193.2 0.1 pad_maximum_fusion
  193.4 0.3 copy.16
  193.7 0.7 copy-done.3
  194.4 0.9 fusion.22
  195.3 0.3 fusion.6
  195.6 1.0 fusion.1
  196.6 0.6 copy-done.1
  197.2 1.6 fusion.11
  198.8 0.8 copy.31
  199.7 31.0 %all-gather.5.cloned.1.call-done = bf16[320,2048]{1,0:T(8,128)(2,1)} async-done(((bf16[80,2048]{1,0:T(8,128)(2,1)}), bf16[320,2048]{1,0:T(8,128)(2,1)}) %all-gather.5.cloned.1.call-update) | async-done | bytes 1310736 | tf_op jit(solution)/shard_map/all_gather | solution.py:75
  230.7 7.0 %convolution_convert_fusion.1 = bf16[320,1792]{1,0:T(8,128)(2,1)} fusion(bf16[320,2048]{1,0:T(8,128)(2,1)} %all-gather.5.cloned.1.call-done, bf16[2048,1792]{1,0:T(8,128)(2,1)} %param.17), kind=kOutput, calls=%fused_computation.7 | convolution fusion | flops 2349383680 | bytes 9797632 | tf_op jit(solution)/shard_map/dot_general | solution.py:74
  237.8 24.7 %reduce-scatter.2.cloned.1.call-done = bf16[80,1792]{1,0:T(8,128)(2,1)} async-done(((bf16[320,1792]{1,0:T(8,128)(2,1)}), bf16[80,1792]{1,0:T(8,128)(2,1)}) %reduce-scatter.2.cloned.1.call-update) | async-done | bytes 286736 | tf_op jit(solution)/shard_map/reduce_scatter | solution.py:79
  (22 shorter events, 0.4 us)
Async XLA Ops:
  7.2 185.6 %copy-start = (bf16[16,128,512]{2,1,0:T(8,128)(2,1)S(1)}, bf16[16,128,512]{2,1,0:T(8,128)(2,1)}, u32[]{:S(2)}) copy-start(bf16[16,128,512]{2,1,0:T(8,128)(2,1)} %param.15) | copy-start | bytes 6291460
  7.2 179.2 %all-gather.3.cloned.1.call-start = ((), (), s32[]{:S(2)}) async-start(), calls=%async_computation.1 | async-start | bytes 11796480 | tf_op jit(solution)/shard_map/all_gather | solution.py:26
  11.4 0.7 copy-start.5
  11.4 0.8 copy-start.6
  11.4 12.2 %copy-start.4 = (bf16[80,576]{1,0:T(8,128)(2,1)S(1)}, bf16[80,576]{1,0:T(8,128)(2,1)}, u32[]{:S(2)}) copy-start(bf16[80,576]{1,0:T(8,128)(2,1)} %param.10) | copy-start | bytes 276484
  11.4 175.0 %copy-start.2 = (bf16[80,1536]{1,0:T(8,128)(2,1)S(1)}, bf16[80,1536]{1,0:T(8,128)(2,1)}, u32[]{:S(2)}) copy-start(bf16[80,1536]{1,0:T(8,128)(2,1)} %param.9) | copy-start | bytes 737284
  11.4 219.3 %all-gather.5.cloned.1.call-start = ((), (), s32[]{:S(2)}) async-start(), calls=%async_computation.2 | async-start | bytes 1638400 | tf_op jit(solution)/shard_map/all_gather | solution.py:75
  193.4 1.0 copy-start.3
  195.6 1.6 copy-start.1
  199.7 62.8 %reduce-scatter.2.cloned.1.call-start = ((), (), s32[]{:S(2)}) async-start(), calls=%async_computation.3 | async-start | bytes 1433600 | tf_op jit(solution)/shard_map/reduce_scatter | solution.py:79
Sparse Core Ops, SparseCore 0:
  11.5 174.7 all-gather.2
  199.8 30.8 all-gather.4
  237.9 24.5 reduce-scatter.1
where the time goes:
time: 269 us
  waiting for transfers between devices  193 us (72%)
  blocking collectives  35 us (13%)
  matrix products  20.6 us (8%)
  between operations  14.5 us (5%)
  local copies, waits for them, and re-layouts  4.87 us (2%)
    all_gather x1, waiting for transfers between devices, on_device(): lax.all_gather(merged_query_weight, 'seq', axis=0, tiled=True)  138 us
    all_gather x1, waiting for transfers between devices, on_device(): lax.all_gather(heads_out, 'seq', axis=0, tiled=True)  31 us
    all_gather x1, blocking collectives, on_device(): key_rows = lax.all_gather(key_value_latents, 'seq', axis=0, tiled=True)  25.1 us
    reduce_scatter x1, waiting for transfers between devices, on_device(): lax.psum_scatter(partial_value.astype(jnp.bfloat16), 'head', scatter_dime...  24.7 us
    unnamed x1, blocking collectives  9.92 us
    dot_general x1, matrix products, on_device(): jnp.dot(lax.all_gather(heads_out, 'seq', axis=0, tiled=True), output_proj...  7.02 us
    dot_general x1, matrix products, on_device(): jnp.dot(query_latent_rows, lax.all_gather(merged_query_weight, 'seq', axi...  5.42 us
  transfers between devices with their start and end apart: 3, of which 3 were waited for; matrix products, arithmetic and copies ran while one was open for 0% of the time, Pallas kernels for 0%

commit v1 on v0

--- a/solution.py
+++ b/solution.py
@@ -23,7 +23,10 @@
     tok_rows = query_latent_rows.shape[0]
     queries = jnp.dot(
         query_latent_rows,
-        lax.all_gather(merged_query_weight, "seq", axis=0, tiled=True),
+        jnp.concatenate(
+            lax.all_to_all(jnp.stack([merged_query_weight] * lax.axis_size("seq")), "seq", 0, 0),
+            axis=0,
+        ),
         preferred_element_type=jnp.float32,
     )
     heads_dev = head_key_up_weight.shape[0]

time: 269 us -> 329 us (1.22)
  blocking collectives: 35 us -> 221 us
  waiting for transfers between devices: 193 us -> 56 us
  starting transfers between devices: 0.12 us -> 6.54 us
  local copies, waits for them, and re-layouts: 4.87 us -> 10.7 us
    unnamed x1, blocking collectives: 9.92 us -> 205 us
    all_gather x1 -> x0, waiting for transfers between devices: 138 us -> none  [on_device(): lax.all_gather(merged_query_weight, 'seq', axis=0, tiled=True)]
    all_gather x1, blocking collectives: 25.1 us -> 15.8 us  [on_device(): key_rows = lax.all_gather(key_value_latents, 'seq', axis=0, tiled=True)]
    all_to_all x0 -> x1, starting transfers between devices: none -> 6.49 us  [on_device(): lax.all_to_all(jnp.stack([merged_query_weight] * lax.axis_size('seq')), '...]
    another operation x0 -> x1, local copies, waits for them, and re-layouts: none -> 5.01 us  [on_device(): jnp.stack([merged_query_weight] * lax.axis_size('seq'))]
  transfers between devices with their start and end apart: 3 -> 3, of which waited for: 3 -> 2; matrix products, arithmetic and copies ran while one was open for 0% -> 0% of each run, Pallas kernels for 0% -> 0%
where the time goes in v1:
time: 329 us
  blocking collectives  221 us (67%)
  waiting for transfers between devices  56 us (17%)
  matrix products  19.3 us (6%)
  between operations  14.8 us (4%)
  local copies, waits for them, and re-layouts  10.7 us (3%)
  starting transfers between devices  6.54 us (2%)
    unnamed x1, blocking collectives  205 us
    all_gather x1, waiting for transfers between devices, on_device(): lax.all_gather(heads_out, 'seq', axis=0, tiled=True)  31.3 us
    reduce_scatter x1, waiting for transfers between devices, on_device(): lax.psum_scatter(partial_value.astype(jnp.bfloat16), 'head', scatter_dime...  24.7 us
    all_gather x1, blocking collectives, on_device(): key_rows = lax.all_gather(key_value_latents, 'seq', axis=0, tiled=True)  15.8 us
    dot_general x1, matrix products, on_device(): jnp.dot(lax.all_gather(heads_out, 'seq', axis=0, tiled=True), output_proj...  7.02 us
  transfers between devices with their start and end apart: 3, of which 2 were waited for; matrix products, arithmetic and copies ran while one was open for 0% of the time, Pallas kernels for 0%

profile of v1, /device:TPU:0, one launch (start us, length us, event | category | flops | bytes accessed | tf_op | source)
XLA Modules:
  0.0 329.0 jit_solution(2136262747963615322)
XLA Ops:
  7.2 2.7 add_convert_fusion
  9.9 1.4 copy-done.1
  11.3 5.0 %stack.2 = bf16[4,384,3072]{2,1,0:T(8,128)(2,1)} broadcast(bf16[384,3072]{1,0:T(8,128)(2,1)S(1)} %add_convert_fusion), dimensions={1,2} | broadcast | bytes 11796480 | tf_op jit(solution)/shard_map/stack | solution.py:27
  16.4 6.5 %all-to-all-start = ((bf16[4,384,3072]{2,1,0:T(8,128)(2,1)}), bf16[4,384,3072]{2,1,0:T(8,128)(2,1)}, u32[]{:S(2)}, u32[]{:S(2)}) async-start(bf16[4,384,3072]{2,1,0:T(8,128)(2,1)} %stack.2), calls=%async_computation | async-start | bytes 18874368 | tf_op jit(solution)/shard_map/all_to_all | solution.py:27
  23.0 0.6 dynamic-slice
  24.3 0.2 dynamic-update-slice
  24.5 205.2 %all-reduce = s32[320]{0:T(512)S(1)} all-reduce(s32[320]{0:T(512)S(1)} %dynamic-update-slice), channel_id=1, replica_groups=mesh['groups'=2,'seq'=4,'head'=4] {'seq'}, use_global_device_ids=true, to_apply=%add | all-reduce | flops 320 | bytes 2560
  229.7 15.8 %all_gather.10 = bf16[320,576]{1,0:T(8,128)(2,1)} all-gather(bf16[80,576]{1,0:T(8,128)(2,1)S(1)} %copy-done.5), channel_id=1, replica_groups=mesh['groups'=2,'seq'=4,'head'=4] {'seq'}, dimensions={0}, use_global_device_ids=true | all-gather | bytes 460800 | tf_op jit(solution)/shard_map/all_gather | solution.py:50
  245.6 5.4 %fusion = bf16[80,3072]{1,0:T(8,128)(2,1)S(1)} fusion(bf16[80,1536]{1,0:T(8,128)(2,1)S(1)} %copy-done.3, bf16[1536,3072]{1,0:T(8,128)(2,1)} %bitcast.1), kind=kOutput, calls=%fused_computation.2 | convolution fusion | flops 755220480 | bytes 10174464 | tf_op jit(solution)/shard_map/dot_general | solution.py:24
  251.0 0.7 reshape.28
  251.9 0.1 copy.20
  252.0 0.5 fusion.3
  252.5 0.1 pad_maximum_fusion
  252.7 0.3 copy.16
  253.0 0.7 copy-done.4
  253.7 0.9 fusion.22
  254.5 0.3 fusion.6
  254.9 1.0 fusion.1
  255.9 0.6 copy-done.2
  256.5 1.7 fusion.11
  258.2 0.8 copy.31
  259.1 31.3 %all-gather.2.cloned.1.call-done = bf16[320,2048]{1,0:T(8,128)(2,1)} async-done(((bf16[80,2048]{1,0:T(8,128)(2,1)}), bf16[320,2048]{1,0:T(8,128)(2,1)}) %all-gather.2.cloned.1.call-update) | async-done | bytes 1310736 | tf_op jit(solution)/shard_map/all_gather | solution.py:78
  290.4 7.0 %convolution_convert_fusion.1 = bf16[320,1792]{1,0:T(8,128)(2,1)} fusion(bf16[320,2048]{1,0:T(8,128)(2,1)} %all-gather.2.cloned.1.call-done, bf16[2048,1792]{1,0:T(8,128)(2,1)} %param.17), kind=kOutput, calls=%fused_computation.7 | convolution fusion | flops 2349383680 | bytes 9797632 | tf_op jit(solution)/shard_map/dot_general | solution.py:77
  297.5 24.7 %reduce-scatter.2.cloned.1.call-done = bf16[80,1792]{1,0:T(8,128)(2,1)} async-done(((bf16[320,1792]{1,0:T(8,128)(2,1)}), bf16[80,1792]{1,0:T(8,128)(2,1)}) %reduce-scatter.2.cloned.1.call-update) | async-done | bytes 286736 | tf_op jit(solution)/shard_map/reduce_scatter | solution.py:82
  (24 shorter events, 0.4 us)
Async XLA Ops:
  7.2 244.8 %copy-start = (bf16[16,128,512]{2,1,0:T(8,128)(2,1)S(1)}, bf16[16,128,512]{2,1,0:T(8,128)(2,1)}, u32[]{:S(2)}) copy-start(bf16[16,128,512]{2,1,0:T(8,128)(2,1)} %param.15) | copy-start | bytes 6291460
  9.9 1.4 copy-start.1
  16.3 6.5 %copy-start.6 = (s32[80]{0:T(128)S(1)}, s32[80]{0:T(128)}, u32[]{:S(2)}) copy-start(s32[80]{0:T(128)} %param.11) | copy-start | bytes 964
  16.3 6.7 %copy-start.7 = (u32[32]{0:T(128)S(1)}, u32[32]{0:T(128)}, u32[]{:S(2)}) copy-start(u32[32]{0:T(128)} %constant.11) | copy-start | bytes 388
  16.3 213.4 %copy-start.5 = (bf16[80,576]{1,0:T(8,128)(2,1)S(1)}, bf16[80,576]{1,0:T(8,128)(2,1)}, u32[]{:S(2)}) copy-start(bf16[80,576]{1,0:T(8,128)(2,1)} %param.10) | copy-start | bytes 276484
  16.4 229.3 %copy-start.3 = (bf16[80,1536]{1,0:T(8,128)(2,1)S(1)}, bf16[80,1536]{1,0:T(8,128)(2,1)}, u32[]{:S(2)}) copy-start(bf16[80,1536]{1,0:T(8,128)(2,1)} %param.9) | copy-start | bytes 737284
  16.4 229.2 %all-to-all-start = ((bf16[4,384,3072]{2,1,0:T(8,128)(2,1)}), bf16[4,384,3072]{2,1,0:T(8,128)(2,1)}, u32[]{:S(2)}, u32[]{:S(2)}) async-start(bf16[4,384,3072]{2,1,0:T(8,128)(2,1)} %stack.2), calls=%async_computation | async-start | bytes 18874368 | tf_op jit(solution)/shard_map/all_to_all | solution.py:27
  22.8 267.6 %all-gather.2.cloned.1.call-start = ((), (), s32[]{:S(2)}) async-start(), calls=%async_computation.2 | async-start | bytes 1638400 | tf_op jit(solution)/shard_map/all_gather | solution.py:78
  252.7 1.0 copy-start.4
  254.9 1.6 copy-start.2
  259.0 63.1 %reduce-scatter.2.cloned.1.call-start = ((), (), s32[]{:S(2)}) async-start(), calls=%async_computation.3 | async-start | bytes 1433600 | tf_op jit(solution)/shard_map/reduce_scatter | solution.py:82
Sparse Core Ops, SparseCore 0:
  259.2 31.2 all-gather.1
  297.6 24.5 reduce-scatter.1
